TPU v7x, 32 devices: a whole 2x2x4 slice. The times are simulated.
32 devices in a mesh: sub: 8 (over z, x), scen: 4 (over y, core).
Axes of the slice: x: 2, y: 2, z: 4, core: 2. Of those that a mesh axis runs over, the one named last changes fastest.
Arguments:
- internal_inverse: bfloat16 [32, 1024, 1024], P('sub', 'scen')
- schur_inverse: bfloat16 [512, 512], P('sub')
- port_nodes: int32 [32, 16], P('sub'), may hold values from 0 to 1023, as said below
- turbine_count: int32 [8], P('sub'), may hold values from 1 to 4, as said below
- partner_port: int32 [512], P('sub'), may hold values from 0 to 511, as said below
- cable_delay: int32 [512], P('sub'), may hold values from 2 to 4, as said below
- history_w: bfloat16 [4, 256, 512], P(None, 'scen', 'sub'), may hold values from -6 to 6
- node_state: float32 [256, 32, 1024], P('scen', 'sub'), may hold values from -6 to 6
- node_gain: float32 [32, 1024], P('sub'), may hold values from 0.02 to 0.3
- stroke_node: int32 [256], P('scen'), may hold values from 0 to 32767, as said below
- stroke_amp: float32 [256], P('scen'), may hold values from 3 to 30
Outputs:
- node_voltage: bfloat16 [256, 32, 1024], P('scen', 'sub')
- cable_waves: bfloat16 [3, 256, 512], P(None, 'scen', 'sub')
Inputs may be any that keep to these rules, and one draw needn't show every extreme that they name: `port_nodes`: the 16 nodes named for one slot are distinct. `turbine_count`: the turbines of one index of sub fill its first slots; the busiest hold all 4. `partner_port`: a cable joins two ports that name each other, of a turbine and the next turbine in slot order (the next used slot, on the same or the next index of sub); a port that names itself has no cable. `cable_delay`: both ends of a cable carry the same delay. `stroke_node`: slot times 1024 plus local node; a stroke on an empty slot injects nothing.
All inputs are finite; a program needn't handle non-finite values.
Results may differ from a plain program's by a relative error of at most 0.004.
The roundings to bfloat16 on the way count: a program that leaves them out, or rounds other values in their place, can miss the bound.
Values may be sent and summed in bfloat16 or wider, within the bound.
A program may use at most 64 MiB of HBM per device.

v0:
```python
import math

import jax
import jax.numpy as jnp
from jax import lax
from jax.sharding import PartitionSpec as P

STEPS = 3


def padded(block, sides, width):
    for axis, dim in sides:
        count = lax.axis_size(axis)
        forward = [(i, i + 1) for i in range(count - 1)]
        backward = [(target, source) for source, target in forward]
        low = lax.ppermute(
            lax.slice_in_dim(block, block.shape[dim] - width, None, axis=dim), axis, forward
        )
        high = lax.ppermute(lax.slice_in_dim(block, 0, width, axis=dim), axis, backward)
        block = jnp.concatenate([low, block, high], axis=dim)
    return block


def per_device(
    internal_inverse,
    schur_inverse,
    port_nodes,
    turbine_count,
    partner_port,
    cable_delay,
    history_w,
    node_state,
    node_gain,
    stroke_node,
    stroke_amp,
):
    slot_count = port_nodes.shape[0]
    port_count = port_nodes.shape[1]
    node_count = internal_inverse.shape[2]
    scen_rows = node_state.shape[0]
    depth = history_w.shape[0]
    if_dev = slot_count * port_count
    device = lax.axis_index("sub")
    slot_used = (jnp.arange(slot_count, dtype=jnp.int32) < turbine_count[0]).astype(jnp.float32)
    port_used = jnp.repeat(slot_used, port_count)
    node_range = jnp.arange(node_count, dtype=jnp.int32)
    port_hot = (port_nodes[:, :, None] == node_range[None, None, :]).astype(jnp.float32)
    node_ids = (device * slot_count + jnp.arange(slot_count, dtype=jnp.int32))[
        :, None
    ] * node_count + node_range[None, :]
    stroke_hot = (stroke_node[:, None, None] == node_ids[None]).astype(jnp.float32)
    own_ports = device * if_dev + jnp.arange(if_dev, dtype=jnp.int32)
    paired = (partner_port != own_ports).astype(jnp.float32)
    partner_col = partner_port - (device - 1) * if_dev
    history_wide = padded(history_w, (("sub", 2),), if_dev)
    hist_cols = jnp.take(history_wide, partner_col, axis=2).astype(jnp.float32)
    schur_wide = schur_inverse.astype(jnp.float32)
    full_inverse = lax.all_gather(internal_inverse, "scen", axis=1, tiled=True)
    port_rows = jnp.take_along_axis(full_inverse, port_nodes[:, :, None], axis=1)
    fresh_cols = jnp.zeros((scen_rows, if_dev), jnp.float32)
    companion = node_state
    wave_list = []
    voltage = jnp.zeros((scen_rows, slot_count, node_count), jnp.float32)
    for step_index in range(STEPS):
        time_now = step_index + 1
        lag_time = time_now - cable_delay
        picked = jnp.zeros((scen_rows, if_dev), jnp.float32)
        for delay_back in range(depth):
            picked = picked + jnp.where(
                (lag_time == -delay_back)[None, :], hist_cols[delay_back], 0.0
            )
        picked = picked + jnp.where((lag_time == 1)[None, :], fresh_cols, 0.0)
        cable_in = -picked * paired[None, :]
        inject = jnp.einsum(
            "sgp,gpn->sgn",
            cable_in.reshape(scen_rows, slot_count, port_count),
            port_hot,
            precision=lax.Precision.HIGHEST,
        )
        wave_value = math.exp(-0.3 * time_now) - math.exp(-2.0 * time_now)
        strike = (stroke_amp * wave_value)[:, None, None] * stroke_hot
        injected = (slot_used[None, :, None] * (companion + strike + inject)).astype(jnp.bfloat16)
        opened = jnp.einsum(
            "sgm,gmn->sgn", injected, full_inverse, preferred_element_type=jnp.float32
        )
        port_open = jnp.take_along_axis(opened, port_nodes[None], axis=2).reshape(scen_rows, if_dev)
        every_port = lax.all_gather(port_open, "sub", axis=1, tiled=True)
        link_current = lax.dot_general(
            every_port,
            schur_wide,
            (((1,), (1,)), ((), ())),
            precision=lax.Precision.HIGHEST,
            preferred_element_type=jnp.float32,
        )
        link_half = link_current.astype(jnp.bfloat16).reshape(scen_rows, slot_count, port_count)
        correction = jnp.einsum(
            "sgp,gpn->sgn", link_half, port_rows, preferred_element_type=jnp.float32
        )
        voltage = slot_used[None, :, None] * (opened - correction)
        companion = -companion - 2.0 * node_gain[None] * voltage
        port_volt = jnp.take_along_axis(voltage, port_nodes[None], axis=2).reshape(
            scen_rows, if_dev
        )
        outgoing = (port_used[None, :] * (0.5 * port_volt + cable_in)).astype(jnp.bfloat16)
        wave_list.append(outgoing)
        if step_index == 0:
            fresh_wide = padded(outgoing, (("sub", 1),), if_dev)
            fresh_cols = jnp.take(fresh_wide, partner_col, axis=1).astype(jnp.float32)
    return (voltage.astype(jnp.bfloat16), jnp.stack(wave_list))


def solution(mesh):
    return jax.shard_map(
        per_device,
        mesh=mesh,
        in_specs=(
            P("sub", "scen", None),
            P("sub", None),
            P("sub", None),
            P("sub"),
            P("sub"),
            P("sub"),
            P(None, "scen", "sub"),
            P("scen", "sub", None),
            P("sub", None),
            P("scen"),
            P("scen"),
        ),
        out_specs=(P("scen", "sub", None), P(None, "scen", "sub")),
        check_vma=False,
    )
```

profile of v0, /device:TPU:0, one launch (start us, length us, event | category | flops | bytes accessed | tf_op | source)
XLA Modules:
  0.0 228.1 jit_solution(14548788545594329199)
XLA Ops:
  7.3 0.7 all-gather.2.cloned.1.call-update
  8.1 0.1 copy.44
  8.2 4.8 %collective-permute-start = (bf16[4,64,64]{1,0,2:T(4,128)(2,1)S(1)}, bf16[4,64,64]{1,0,2:T(4,128)(2,1)S(1)}, u32[]{:S(2)}, u32[]{:S(2)}) collective-permute-start(bf16[4,64,64]{1,0,2:T(4,128)(2,1)S(1)} %copy.44), channel_id=1, source_target_pairs={{0,4},{4,8},{8,12},{12,16},{16,20},{20,24},{24,28},{1,5},{5,9},{9,... | collective-permute-start | bytes 98312 | tf_op jit(solution)/shard_map/ppermute | solution.py:16
  13.0 1.3 collective-permute-start.1
  15.2 0.6 broadcast_multiply_fusion.1
  16.0 0.6 broadcast_multiply_fusion
  17.0 0.1 reshape.565
  17.2 0.6 mul.248
  17.9 0.6 broadcast_in_dim.277
  18.5 0.6 broadcast_in_dim.267
  19.1 0.6 broadcast_in_dim.269
  19.6 0.7 broadcast_in_dim.271
  20.3 0.6 broadcast_in_dim.273
  20.9 0.6 broadcast_in_dim.275
  21.5 0.7 broadcast_in_dim.286
  22.2 0.6 broadcast_in_dim.288
  22.8 0.6 broadcast_in_dim.290
  23.4 0.6 broadcast_in_dim.292
  24.0 0.7 broadcast_in_dim.294
  24.7 0.2 pad_maximum_fusion
  24.9 0.7 gather_fusion
  25.6 0.1 convert_bitcast_fusion
  25.7 0.1 fusion.99
  25.9 1.3 fusion.12
  27.2 43.5 %all-gather.2.cloned.1.call-done = bf16[4,1024,1024]{2,1,0:T(8,128)(2,1)} async-done(((bf16[4,256,1024]{2,1,0:T(8,128)(2,1)}), bf16[4,1024,1024]{2,1,0:T(8,128)(2,1)}) %all-gather.2.cloned.1.call-update) | async-done | bytes 8388624 | tf_op jit(solution)/shard_map/all_gather | solution.py:58
  70.7 5.0 %convolution_bitcast_fusion.7 = f32[64,4,1024]{2,0,1:T(8,128)S(1)} fusion(bf16[64,4,1024]{2,0,1:T(8,128)(2,1)S(1)} %fusion.12, bf16[4,1024,1024]{2,1,0:T(8,128)(2,1)} %all-gather.2.cloned.1.call-done), kind=kOutput, calls=%fused_computation.29 | convolution fusion | flops 536870912 | bytes 9961472 | tf_op jit(solution)/shard_map/sgm,gmn->sgn/dot_general | solution.py:83
  75.8 1.9 copy.47
  77.8 1.5 gather_fusion.3
  79.3 30.8 %all_gather.13 = f32[64,512]{0,1:T(8,128)S(1)} all-gather(f32[64,64]{0,1:T(8,128)S(1)} %bitcast.170), channel_id=1, replica_groups=mesh['sub'=8,'scen'=4] {'sub'}, dimensions={1}, use_global_device_ids=true | all-gather | bytes 147456 | tf_op jit(solution)/shard_map/all_gather | solution.py:87
  110.1 0.4 convolution_convert_fusion.2
  110.5 0.1 copy.48
  110.6 1.7 gather_fusion.2
  112.4 0.3 fusion.9
  112.7 0.6 copy.49
  113.3 0.9 gather_fusion.4
  114.3 0.9 fusion.45
  115.2 3.4 %collective-permute-start.2 = (bf16[64,64]{0,1:T(8,128)(2,1)S(1)}, bf16[64,64]{0,1:T(8,128)(2,1)S(1)}, u32[]{:S(2)}, u32[]{:S(2)}) collective-permute-start(bf16[64,64]{0,1:T(8,128)(2,1)S(1)} %fusion.45), channel_id=1, source_target_pairs={{0,4},{4,8},{8,12},{12,16},{16,20},{20,24},{24,28},{1,5},{5,9},{9,... | collective-permute-start | bytes 24584 | tf_op jit(solution)/shard_map/ppermute | solution.py:16
  118.6 1.3 collective-permute-start.3
  119.9 2.0 multiply_convert_fusion.2
  121.9 2.3 %collective-permute-done.3 = bf16[64,64]{0,1:T(8,128)(2,1)S(1)} collective-permute-done((bf16[64,64]{0,1:T(8,128)(2,1)S(1)}, bf16[64,64]{0,1:T(8,128)(2,1)S(1)}, u32[]{:S(2)}, u32[]{:S(2)}) %collective-permute-start.3) | collective-permute-done | bytes 8224 | tf_op jit(solution)/shard_map/ppermute | solution.py:19
  124.3 0.8 gather_fusion.1
  125.0 2.8 %fusion.13 = bf16[64,4,1024]{2,0,1:T(8,128)(2,1)S(1)} fusion(f32[64]{0:T(128)} %get-tuple-element.35, s32[4,1024]{1,0:T(4,128)} %copy-done.14, f32[4]{0:T(128)} %copy-done.21, s32[64]{0:T(128)} %param.22, f32[64,4,1024]{2,0,1:T(8,128)S(1)} %fusion.9, f32[4,1024]{1,0:T(4,128)} %broadcast_multiply_fusion, f32[64,4,1024]{2,1,0:T(4,128)} %param.20, ...), kind=kOutput, calls=%fused_computation.34 | convolution fusion | flops 52809728 | bytes 2729360 | tf_op jit(solution)/shard_map/sgp,gpn->sgn/dot_general | solution.py:74
  127.8 5.0 %convolution_bitcast_fusion.4 = f32[64,4,1024]{2,0,1:T(8,128)S(1)} fusion(bf16[64,4,1024]{2,0,1:T(8,128)(2,1)S(1)} %fusion.13, bf16[4,1024,1024]{2,1,0:T(8,128)(2,1)} %all-gather.2.cloned.1.call-done), kind=kOutput, calls=%fused_computation.22 | convolution fusion | flops 536870912 | bytes 9961472 | tf_op jit(solution)/shard_map/sgm,gmn->sgn/dot_general | solution.py:83
  132.8 1.9 copy.50
  134.7 1.5 gather_fusion.5
  136.3 30.9 %all_gather.14 = f32[64,512]{0,1:T(8,128)S(1)} all-gather(f32[64,64]{0,1:T(8,128)S(1)} %bitcast.171), channel_id=1, replica_groups=mesh['sub'=8,'scen'=4] {'sub'}, dimensions={1}, use_global_device_ids=true | all-gather | bytes 147456 | tf_op jit(solution)/shard_map/all_gather | solution.py:87
  167.2 0.4 convolution_convert_fusion.1
  167.7 1.0 fusion.5
  168.9 1.9 copy.54
  170.9 2.8 %fusion.14 = bf16[64,4,1024]{2,0,1:T(8,128)(2,1)S(1)} fusion(f32[64,4,1024]{2,0,1:T(8,128)S(1)} %fusion.5, f32[64]{0:T(128)S(1)} %copy-done.35, s32[4,1024]{1,0:T(4,128)S(1)} %copy-done.15, f32[4,1024]{1,0:T(4,128)S(1)} %copy-done.16, f32[4]{0:T(128)S(1)} %copy-done.22, s32[64]{0:T(128)S(1)} %copy-done.57, f32[64,4,1024]{2,0,1:T(8,128)S(1)} %fusion.9, ...), kind=kOutput, calls=%fused_computation.35 | convolution fusion | flops 53596160 | bytes 3777936 | tf_op jit(solution)/shard_map/sgp,gpn->sgn/dot_general | solution.py:74
  173.7 5.0 %convolution_bitcast_fusion.1 = f32[64,4,1024]{2,0,1:T(8,128)S(1)} fusion(bf16[64,4,1024]{2,0,1:T(8,128)(2,1)S(1)} %fusion.14, bf16[4,1024,1024]{2,1,0:T(8,128)(2,1)} %all-gather.2.cloned.1.call-done), kind=kOutput, calls=%fused_computation.15 | convolution fusion | flops 536870912 | bytes 9961472 | tf_op jit(solution)/shard_map/sgm,gmn->sgn/dot_general | solution.py:83
  178.7 0.6 copy.52
  179.3 0.9 gather_fusion.6
  180.3 30.7 %all_gather.15 = f32[64,512]{0,1:T(8,128)S(1)} all-gather(f32[64,64]{0,1:T(8,128)S(1)} %bitcast.172), channel_id=1, replica_groups=mesh['sub'=8,'scen'=4] {'sub'}, dimensions={1}, use_global_device_ids=true | all-gather | bytes 147456 | tf_op jit(solution)/shard_map/all_gather | solution.py:87
  211.0 0.4 convolution_convert_fusion
  211.5 1.2 fusion.100
  212.7 1.9 copy.57
  214.7 1.5 gather_fusion.8
  216.2 0.9 gather_fusion.7
  217.3 0.9 multiply_convert_fusion.1
  218.2 0.9 multiply_convert_fusion
  219.2 0.1 pad_maximum_fusion.1
  219.3 0.7 copy.59
  220.1 1.2 copy.58
  (161 shorter events, 1.7 us)
Async XLA Ops:
  7.2 102.9 %copy-start = (bf16[64,512]{1,0:T(8,128)(2,1)S(1)}, bf16[64,512]{1,0:T(8,128)(2,1)}, u32[]{:S(2)}) copy-start(bf16[64,512]{1,0:T(8,128)(2,1)} %param.14) | copy-start | bytes 196612
  7.2 7.8 %copy-start.65 = (s32[64]{0:T(128)S(1)}, s32[64]{0:T(128)}, u32[]{:S(2)}) copy-start(s32[64]{0:T(128)} %param.17) | copy-start | bytes 772
  7.2 7.8 %copy-start.66 = (s32[64]{0:T(128)S(1)}, s32[64]{0:T(128)}, u32[]{:S(2)}) copy-start(s32[64]{0:T(128)} %param.18) | copy-start | bytes 772
  7.2 8.0 %copy-start.64 = (f32[64]{0:T(128)S(1)}, f32[64]{0:T(128)}, u32[]{:S(2)}) copy-start(f32[64]{0:T(128)} %param.23) | copy-start | bytes 772
  7.2 8.6 %copy-start.18 = (s32[4,16]{1,0:T(4,128)S(1)}, s32[4,16]{1,0:T(4,128)}, u32[]{:S(2)}) copy-start(s32[4,16]{1,0:T(4,128)} %param.15) | copy-start | bytes 772
  7.2 8.7 %copy-start.19 = (f32[4,1024]{1,0:T(4,128)S(1)}, f32[4,1024]{1,0:T(4,128)}, u32[]{:S(2)}) copy-start(f32[4,1024]{1,0:T(4,128)} %param.21) | copy-start | bytes 49156
  7.2 18.6 %copy-start.3 = (f32[64,4,1024]{2,1,0:T(4,128)S(1)}, f32[64,4,1024]{2,1,0:T(4,128)}, u32[]{:S(2)}) copy-start(f32[64,4,1024]{2,1,0:T(4,128)} %param.20) | copy-start | bytes 3145732
  7.3 18.6 %copy-start.56 = (s32[64]{0:T(128)S(1)}, s32[64]{0:T(128)}, u32[]{:S(2)}) copy-start(s32[64]{0:T(128)} %param.22) | copy-start | bytes 772
  7.3 63.4 %all-gather.2.cloned.1.call-start = ((), (), s32[]{:S(2)}) async-start(), calls=%async_computation | async-start | bytes 10485760 | tf_op jit(solution)/shard_map/all_gather | solution.py:58
  8.2 16.5 %collective-permute-start = (bf16[4,64,64]{1,0,2:T(4,128)(2,1)S(1)}, bf16[4,64,64]{1,0,2:T(4,128)(2,1)S(1)}, u32[]{:S(2)}, u32[]{:S(2)}) collective-permute-start(bf16[4,64,64]{1,0,2:T(4,128)(2,1)S(1)} %copy.44), channel_id=1, source_target_pairs={{0,4},{4,8},{8,12},{12,16},{16,20},{20,24},{24,28},{1,5},{5,9},{9,... | collective-permute-start | bytes 98312 | tf_op jit(solution)/shard_map/ppermute | solution.py:16
  13.0 11.7 %collective-permute-start.1 = (bf16[4,64,64]{1,0,2:T(4,128)(2,1)S(1)}, bf16[4,64,64]{1,0,2:T(4,128)(2,1)S(1)}, u32[]{:S(2)}, u32[]{:S(2)}) collective-permute-start(bf16[4,64,64]{1,0,2:T(4,128)(2,1)S(1)} %copy.44), channel_id=1, source_target_pairs={{4,0},{8,4},{12,8},{16,12},{20,16},{24,20},{28,24},{5,1},{9,5},{13... | collective-permute-start | bytes 98312 | tf_op jit(solution)/shard_map/ppermute | solution.py:19
  15.1 10.5 %copy-start.40 = (pred[64]{0:T(512)(128)(4,1)}, pred[64]{0:T(512)(128)(4,1)S(1)}, u32[]{:S(2)}) copy-start(pred[64]{0:T(512)(128)(4,1)S(1)} %get-tuple-element.50) | copy-start | bytes 196
  15.1 10.5 %copy-start.42 = (pred[64]{0:T(512)(128)(4,1)}, pred[64]{0:T(512)(128)(4,1)S(1)}, u32[]{:S(2)}) copy-start(pred[64]{0:T(512)(128)(4,1)S(1)} %get-tuple-element.51) | copy-start | bytes 196
  15.1 10.5 %copy-start.44 = (pred[64]{0:T(512)(128)(4,1)}, pred[64]{0:T(512)(128)(4,1)S(1)}, u32[]{:S(2)}) copy-start(pred[64]{0:T(512)(128)(4,1)S(1)} %get-tuple-element.52) | copy-start | bytes 196
  15.1 10.5 %copy-start.46 = (pred[64]{0:T(512)(128)(4,1)}, pred[64]{0:T(512)(128)(4,1)S(1)}, u32[]{:S(2)}) copy-start(pred[64]{0:T(512)(128)(4,1)S(1)} %get-tuple-element.39) | copy-start | bytes 196
  15.1 10.5 %copy-start.48 = (pred[64]{0:T(512)(128)(4,1)}, pred[64]{0:T(512)(128)(4,1)S(1)}, u32[]{:S(2)}) copy-start(pred[64]{0:T(512)(128)(4,1)S(1)} %get-tuple-element.44) | copy-start | bytes 196
  15.1 10.5 %copy-start.50 = (pred[64]{0:T(512)(128)(4,1)}, pred[64]{0:T(512)(128)(4,1)S(1)}, u32[]{:S(2)}) copy-start(pred[64]{0:T(512)(128)(4,1)S(1)} %get-tuple-element.45) | copy-start | bytes 196
  15.1 10.5 %copy-start.52 = (pred[64]{0:T(512)(128)(4,1)}, pred[64]{0:T(512)(128)(4,1)S(1)}, u32[]{:S(2)}) copy-start(pred[64]{0:T(512)(128)(4,1)S(1)} %get-tuple-element.46) | copy-start | bytes 196
  15.1 10.5 %copy-start.54 = (pred[64]{0:T(512)(128)(4,1)}, pred[64]{0:T(512)(128)(4,1)S(1)}, u32[]{:S(2)}) copy-start(pred[64]{0:T(512)(128)(4,1)S(1)} %get-tuple-element.47) | copy-start | bytes 196
  15.1 60.6 %copy-start.24 = (pred[64]{0:T(512)(128)(4,1)}, pred[64]{0:T(512)(128)(4,1)S(1)}, u32[]{:S(2)}) copy-start(pred[64]{0:T(512)(128)(4,1)S(1)} %get-tuple-element.9) | copy-start | bytes 196
  15.1 60.6 %copy-start.32 = (pred[64]{0:T(512)(128)(4,1)}, pred[64]{0:T(512)(128)(4,1)S(1)}, u32[]{:S(2)}) copy-start(pred[64]{0:T(512)(128)(4,1)S(1)} %get-tuple-element.41) | copy-start | bytes 196
  15.2 60.6 %copy-start.33 = (pred[64]{0:T(512)(128)(4,1)}, pred[64]{0:T(512)(128)(4,1)S(1)}, u32[]{:S(2)}) copy-start(pred[64]{0:T(512)(128)(4,1)S(1)} %get-tuple-element.42) | copy-start | bytes 196
  15.2 60.6 %copy-start.34 = (pred[64]{0:T(512)(128)(4,1)}, pred[64]{0:T(512)(128)(4,1)S(1)}, u32[]{:S(2)}) copy-start(pred[64]{0:T(512)(128)(4,1)S(1)} %get-tuple-element.43) | copy-start | bytes 196
  15.2 60.6 %copy-start.36 = (pred[64]{0:T(512)(128)(4,1)}, pred[64]{0:T(512)(128)(4,1)S(1)}, u32[]{:S(2)}) copy-start(pred[64]{0:T(512)(128)(4,1)S(1)} %get-tuple-element.48) | copy-start | bytes 196
  15.2 60.6 %copy-start.38 = (pred[64]{0:T(512)(128)(4,1)}, pred[64]{0:T(512)(128)(4,1)S(1)}, u32[]{:S(2)}) copy-start(pred[64]{0:T(512)(128)(4,1)S(1)} %get-tuple-element.49) | copy-start | bytes 196
  15.2 60.5 %copy-start.30 = (s32[1024]{0:T(1024)}, s32[1024]{0:T(1024)S(1)}, u32[]{:S(2)}) copy-start(s32[1024]{0:T(1024)S(1)} %pad_clamp_fusion) | copy-start | bytes 12292
  15.9 96.5 %copy-start.28 = (pred[4,16]{1,0:T(4,128)(4,1)}, pred[4,16]{1,0:T(4,128)(4,1)S(1)}, u32[]{:S(2)}) copy-start(pred[4,16]{1,0:T(4,128)(4,1)S(1)} %compare_and_fusion) | copy-start | bytes 196
  16.0 59.8 %copy-start.14 = (s32[4,1024]{1,0:T(4,128)}, s32[4,1024]{1,0:T(4,128)S(1)}, u32[]{:S(2)}) copy-start(s32[4,1024]{1,0:T(4,128)S(1)} %iota_add_fusion) | copy-start | bytes 49156
  16.6 95.8 %copy-start.21 = (f32[4]{0:T(128)}, f32[4]{0:T(128)S(1)}, u32[]{:S(2)}) copy-start(f32[4]{0:T(128)S(1)} %compare_convert_fusion.1) | copy-start | bytes 52
  16.6 59.1 %copy-start.26 = (f32[4,16]{1,0:T(4,128)}, f32[4,16]{1,0:T(4,128)S(1)}, u32[]{:S(2)}) copy-start(f32[4,16]{1,0:T(4,128)S(1)} %mul.238) | copy-start | bytes 772
  25.8 50.0 %copy-start.4 = (f32[1,64,64]{1,0,2:T(1,128)}, f32[1,64,64]{1,0,2:T(1,128)S(1)}, u32[]{:S(2)}) copy-start(f32[1,64,64]{1,0,2:T(1,128)S(1)} %get-tuple-element.12) | copy-start | bytes 49156
  25.9 50.0 %copy-start.6 = (f32[1,64,64]{1,0,2:T(1,128)}, f32[1,64,64]{1,0,2:T(1,128)S(1)}, u32[]{:S(2)}) copy-start(f32[1,64,64]{1,0,2:T(1,128)S(1)} %get-tuple-element.13) | copy-start | bytes 49156
  25.9 49.9 %copy-start.8 = (f32[1,64,64]{1,0,2:T(1,128)}, f32[1,64,64]{1,0,2:T(1,128)S(1)}, u32[]{:S(2)}) copy-start(f32[1,64,64]{1,0,2:T(1,128)S(1)} %get-tuple-element.14) | copy-start | bytes 49156
  115.2 6.7 %collective-permute-start.2 = (bf16[64,64]{0,1:T(8,128)(2,1)S(1)}, bf16[64,64]{0,1:T(8,128)(2,1)S(1)}, u32[]{:S(2)}, u32[]{:S(2)}) collective-permute-start(bf16[64,64]{0,1:T(8,128)(2,1)S(1)} %fusion.45), channel_id=1, source_target_pairs={{0,4},{4,8},{8,12},{12,16},{16,20},{20,24},{24,28},{1,5},{5,9},{9,... | collective-permute-start | bytes 24584 | tf_op jit(solution)/shard_map/ppermute | solution.py:16
  118.6 5.6 %collective-permute-start.3 = (bf16[64,64]{0,1:T(8,128)(2,1)S(1)}, bf16[64,64]{0,1:T(8,128)(2,1)S(1)}, u32[]{:S(2)}, u32[]{:S(2)}) collective-permute-start(bf16[64,64]{0,1:T(8,128)(2,1)S(1)} %fusion.45), channel_id=1, source_target_pairs={{4,0},{8,4},{12,8},{16,12},{20,16},{24,20},{28,24},{5,1},{9,5},{13... | collective-permute-start | bytes 24584 | tf_op jit(solution)/shard_map/ppermute | solution.py:19
  125.0 7.8 %copy-start.10 = (bf16[64,64]{1,0:T(8,128)(2,1)}, bf16[64,64]{1,0:T(8,128)(2,1)S(1)}, u32[]{:S(2)}) copy-start(bf16[64,64]{1,0:T(8,128)(2,1)S(1)} %gather_fusion.1) | copy-start | bytes 24580
  168.7 2.1 copy-start.5
  168.7 2.1 copy-start.7
  168.7 2.1 copy-start.9
  168.8 2.1 copy-start.11
  168.8 2.1 copy-start.15
  168.8 2.1 copy-start.16
  168.8 2.1 copy-start.22
  168.8 2.1 copy-start.27
  168.8 2.1 copy-start.35
  168.8 2.1 copy-start.57
  178.7 32.8 %copy-start.23 = (f32[4]{0:T(128)S(1)}, f32[4]{0:T(128)}, u32[]{:S(2)}) copy-start(f32[4]{0:T(128)} %copy-done.21) | copy-start | bytes 52
  178.7 32.8 %copy-start.29 = (pred[4,16]{1,0:T(4,128)(4,1)S(1)}, pred[4,16]{1,0:T(4,128)(4,1)}, u32[]{:S(2)}) copy-start(pred[4,16]{1,0:T(4,128)(4,1)} %copy-done.28) | copy-start | bytes 196
  212.7 3.5 %copy-start.1 = (f32[64,4,1024]{0,2,1:T(8,128)S(1)}, f32[64,4,1024]{0,2,1:T(8,128)}, u32[]{:S(2)}) copy-start(f32[64,4,1024]{0,2,1:T(8,128)} %copy.54) | copy-start | bytes 3145732
  212.7 4.5 %copy-start.12 = (bf16[64,64]{1,0:T(8,128)(2,1)S(1)}, bf16[64,64]{1,0:T(8,128)(2,1)}, u32[]{:S(2)}) copy-start(bf16[64,64]{1,0:T(8,128)(2,1)} %copy-done.10) | copy-start | bytes 24580
  212.7 4.5 %copy-start.20 = (f32[64]{0:T(128)S(1)}, f32[64]{0:T(128)}, u32[]{:S(2)}) copy-start(f32[64]{0:T(128)} %mul.248) | copy-start | bytes 772
  212.7 4.5 %copy-start.25 = (pred[64]{0:T(512)(128)(4,1)S(1)}, pred[64]{0:T(512)(128)(4,1)}, u32[]{:S(2)}) copy-start(pred[64]{0:T(512)(128)(4,1)} %copy-done.24) | copy-start | bytes 196
  212.7 4.5 %copy-start.47 = (pred[64]{0:T(512)(128)(4,1)S(1)}, pred[64]{0:T(512)(128)(4,1)}, u32[]{:S(2)}) copy-start(pred[64]{0:T(512)(128)(4,1)} %copy-done.46) | copy-start | bytes 196
  212.7 4.5 %copy-start.49 = (pred[64]{0:T(512)(128)(4,1)S(1)}, pred[64]{0:T(512)(128)(4,1)}, u32[]{:S(2)}) copy-start(pred[64]{0:T(512)(128)(4,1)} %copy-done.48) | copy-start | bytes 196
  212.7 4.5 %copy-start.51 = (pred[64]{0:T(512)(128)(4,1)S(1)}, pred[64]{0:T(512)(128)(4,1)}, u32[]{:S(2)}) copy-start(pred[64]{0:T(512)(128)(4,1)} %copy-done.50) | copy-start | bytes 196
  212.7 4.5 %copy-start.53 = (pred[64]{0:T(512)(128)(4,1)S(1)}, pred[64]{0:T(512)(128)(4,1)}, u32[]{:S(2)}) copy-start(pred[64]{0:T(512)(128)(4,1)} %copy-done.52) | copy-start | bytes 196
  212.7 4.5 %copy-start.55 = (pred[64]{0:T(512)(128)(4,1)S(1)}, pred[64]{0:T(512)(128)(4,1)}, u32[]{:S(2)}) copy-start(pred[64]{0:T(512)(128)(4,1)} %copy-done.54) | copy-start | bytes 196
  214.7 3.5 %copy-start.37 = (pred[64]{0:T(512)(128)(4,1)S(1)}, pred[64]{0:T(512)(128)(4,1)}, u32[]{:S(2)}) copy-start(pred[64]{0:T(512)(128)(4,1)} %copy-done.36) | copy-start | bytes 196
  214.7 3.5 %copy-start.39 = (pred[64]{0:T(512)(128)(4,1)S(1)}, pred[64]{0:T(512)(128)(4,1)}, u32[]{:S(2)}) copy-start(pred[64]{0:T(512)(128)(4,1)} %copy-done.38) | copy-start | bytes 196
  214.7 3.5 %copy-start.41 = (pred[64]{0:T(512)(128)(4,1)S(1)}, pred[64]{0:T(512)(128)(4,1)}, u32[]{:S(2)}) copy-start(pred[64]{0:T(512)(128)(4,1)} %copy-done.40) | copy-start | bytes 196
  214.7 3.6 %copy-start.43 = (pred[64]{0:T(512)(128)(4,1)S(1)}, pred[64]{0:T(512)(128)(4,1)}, u32[]{:S(2)}) copy-start(pred[64]{0:T(512)(128)(4,1)} %copy-done.42) | copy-start | bytes 196
  214.7 3.6 %copy-start.45 = (pred[64]{0:T(512)(128)(4,1)S(1)}, pred[64]{0:T(512)(128)(4,1)}, u32[]{:S(2)}) copy-start(pred[64]{0:T(512)(128)(4,1)} %copy-done.44) | copy-start | bytes 196
  214.7 4.5 %copy-start.13 = (bf16[1,64,64]{1,0,2:T(2,128)(2,1)S(1)}, bf16[1,64,64]{1,0,2:T(2,128)(2,1)}, u32[]{:S(2)}) copy-start(bf16[1,64,64]{1,0,2:T(2,128)(2,1)} %multiply_convert_fusion.2) | copy-start | bytes 24580
  214.7 5.4 %copy-start.2 = (bf16[64,4,1024]{2,0,1:T(8,128)(2,1)S(1)}, bf16[64,4,1024]{2,0,1:T(8,128)(2,1)}, u32[]{:S(2)}) copy-start(bf16[64,4,1024]{2,0,1:T(8,128)(2,1)} %get-tuple-element.37) | copy-start | bytes 1572868
  (8 other events, 15.2 us)
Sparse Core Ops, SparseCore 0:
  9.7 60.9 all-gather.1
where the time goes:
time: 229 us; the launch traced here: 228 us
  blocking collectives  92.5 us (40%)
  waiting for transfers between devices  46.5 us (20%)
  local copies, waits for them, and re-layouts  30 us (13%)
  matrix products  25.5 us (11%)
  between operations  15.8 us (7%)
  starting transfers between devices  10.9 us (5%)
  other arithmetic  6.98 us (3%)
    all_gather x3, blocking collectives, per_device(): every_port = lax.all_gather(port_open, 'sub', axis=1, tiled=True)  92.5 us
    all_gather x1, waiting for transfers between devices, per_device(): full_inverse = lax.all_gather(internal_inverse, 'scen', axis=1, tiled=True)  43.5 us
    dot_general x3, matrix products, per_device(): jnp.einsum('sgm,gmn->sgn', injected, full_inverse, preferred_element_type...  15 us
    ppermute x2, starting transfers between devices, padded(): lax.ppermute(lax.slice_in_dim(block, block.shape[dim] - width, None, axis...  8.24 us
    dot_general x3, matrix products, per_device(): jnp.einsum('sgp,gpn->sgn', cable_in.reshape(scen_rows, slot_count, port_c...  6.85 us
    broadcast_in_dim x12, local copies, waits for them, and re-layouts, per_device(): jnp.where((lag_time == -delay_back)[None, :], hist_cols[delay_back], 0.0)  5.29 us
    convert_element_type x4, other arithmetic, per_device(): (port_used[None, :] * (0.5 * port_volt + cable_in)).astype(jnp.bfloat16)  4.8 us
  transfers between devices with their start and end apart: 5, of which 2 were waited for; matrix products, arithmetic and copies ran while one was open for 6% of the time, Pallas kernels for 0%

commit v1 on v0

v1 whole, which is shorter than its diff:
```python
import functools
import math

import jax
import jax.numpy as jnp
from jax import lax
from jax.experimental import pallas as pl
from jax.experimental.pallas import tpu as pltpu
from jax.sharding import PartitionSpec as P

STEPS = 3
SPLIT = 2
F32 = jnp.float32
BF16 = jnp.bfloat16
MESH = pl.DeviceIdType.MESH


def dot(left, right):
    return jnp.dot(left, right, preferred_element_type=F32)


def dot_t(left, right):
    return lax.dot_general(left, right, (((1,), (1,)), ((), ())), preferred_element_type=F32)


def kernel(
    n_sub,
    inv,
    schur,
    port_nodes,
    turbine_count,
    partner,
    delay,
    hist,
    node_state,
    gain,
    stroke_node,
    stroke_amp,
    volt_out,
    wave_out,
    full,
    state_in,
    companion,
    opened,
    lhs,
    prow,
    pct,
    pcb,
    gbuf,
    sbuf,
    hbuf,
    fbuf,
    own_sem,
    state_sem,
    w_send,
    w_recv,
    pc_send,
    pc_recv,
    h_send,
    h_recv,
    f_send,
    f_recv,
    g_send,
    g_recv,
):
    slots, rows, nodes = inv.shape
    ports = port_nodes.shape[1]
    scens = hist.shape[1]
    iface = slots * ports
    depth = hist.shape[0]
    width = 2 * iface
    part = rows // SPLIT
    me = lax.axis_index("scen")
    dev = lax.axis_index("sub")
    sib = me + 1 - 2 * lax.rem(me, 2)
    across = lax.rem(me + 2, 4)
    diag = 3 - me
    right = lax.rem(dev + 1, n_sub)
    left = lax.rem(dev + n_sub - 1, n_sub)

    own_copy = pltpu.make_async_copy(inv, full.at[:, pl.ds(me * rows, rows), :], own_sem)
    own_copy.start()
    state_copy = pltpu.make_async_copy(node_state, state_in, state_sem)
    state_copy.start()

    barrier = pltpu.get_barrier_semaphore()
    for peer in (across, sib, diag):
        pl.semaphore_signal(barrier, inc=1, device_id={"scen": peer}, device_id_type=MESH)

    def greet(offset, carry):
        pl.semaphore_signal(
            barrier,
            inc=1,
            device_id={"sub": lax.rem(dev + offset, n_sub)},
            device_id_type=MESH,
        )
        return carry

    lax.fori_loop(1, n_sub, greet, 0)
    pl.semaphore_wait(barrier, n_sub + 2)

    def remote(src, dst, send, recv, peer):
        return pltpu.make_async_remote_copy(
            src_ref=src,
            dst_ref=dst,
            send_sem=send,
            recv_sem=recv,
            device_id=peer,
            device_id_type=MESH,
        )

    def block(g, owner, piece):
        return full.at[g, pl.ds(owner * rows + piece * part, part), :]

    def weight_send(which, peer, g, piece):
        return remote(
            inv.at[g, pl.ds(piece * part, part), :],
            block(g, me, piece),
            w_send.at[which, g, piece],
            w_recv.at[which, g, piece],
            {"scen": peer},
        )

    def forward(g, piece):
        return remote(
            block(g, across, piece),
            block(g, across, piece),
            w_send.at[2, g, piece],
            w_recv.at[2, g, piece],
            {"scen": sib},
        )

    def forwarded(g, piece):
        return remote(
            block(g, diag, piece),
            block(g, diag, piece),
            w_send.at[2, g, piece],
            w_recv.at[2, g, piece],
            {"scen": sib},
        )

    def send_slot(g, carry):
        for piece in range(SPLIT):
            weight_send(0, across, g, piece).start()
        for piece in range(SPLIT):
            weight_send(1, sib, g, piece).start()
        return carry

    weight_send(0, across, 0, 0).start()

    def hist_send(side, peer):
        return remote(hist, hbuf.at[side], h_send.at[side], h_recv.at[side], {"sub": peer})

    hist_send(0, right).start()
    hist_send(1, left).start()

    def column(row, count):
        eye = lax.broadcasted_iota(jnp.int32, (count, count), 0) == lax.broadcasted_iota(
            jnp.int32, (count, count), 1
        )
        return jnp.sum(jnp.where(eye, row, jnp.zeros_like(row)), axis=1, keepdims=True)

    node_row = lax.broadcasted_iota(jnp.int32, (1, nodes), 1)
    hots = []
    for g in range(slots):
        col = column(port_nodes[g : g + 1, :].astype(F32), ports)
        hots.append((col == node_row.astype(F32)).astype(F32))
    hot_all = jnp.concatenate(hots, axis=0)
    slot_col = lax.broadcasted_iota(jnp.int32, (iface, 1), 0) // ports
    for g in range(slots):
        lhs[g, scens:, :] = (hot_all * (slot_col == g).astype(F32)).astype(BF16)
    hot_all = hot_all.astype(BF16)

    own_copy.wait()

    def own_cols(g, total):
        return total + dot_t(lhs[g, scens:, :], full[g, pl.ds(me * rows, rows), :])

    cols = lax.fori_loop(0, slots, own_cols, jnp.zeros((iface, rows), F32))
    my_cols = pct.at[:, pl.ds(pl.multiple_of(me * rows, rows), rows)]
    my_cols[...] = cols.astype(BF16)

    def pc_copy(which, owner, peer):
        cols_ref = pct.at[:, pl.ds(pl.multiple_of(owner * rows, rows), rows)]
        return remote(cols_ref, cols_ref, pc_send.at[which], pc_recv.at[which], {"scen": peer})

    for which, peer in enumerate((across, sib, diag)):
        pc_copy(which, me, peer).start()
    for piece in range(1, SPLIT):
        weight_send(0, across, 0, piece).start()
    for piece in range(SPLIT):
        weight_send(1, sib, 0, piece).start()
    lax.fori_loop(1, slots, send_slot, 0)

    used_row = (
        lax.broadcasted_iota(jnp.int32, (1, iface), 1) // ports < turbine_count[0]
    ).astype(F32)
    stroke_col = column(stroke_node[...].astype(F32), scens)
    amp_col = column(stroke_amp[...], scens)
    port_lane = lax.broadcasted_iota(jnp.int32, (1, iface), 1)
    partner_row = partner[...]
    delay_row = delay[...]
    paired = (partner_row != port_lane + dev * iface).astype(F32)
    port_sub = lax.broadcasted_iota(jnp.int32, (iface, 1), 0)
    picks = [
        (partner_row == port_sub + (dev + shift) * iface).astype(F32) * paired
        for shift in (-1, 0, 1)
    ]

    def pick(blocks, lag):
        chosen = (delay_row == lag).astype(F32)
        return sum(dot(b, (m * chosen).astype(BF16)) for b, m in zip(blocks, picks))

    for o in range(n_sub):
        piece = schur[:, o * iface : (o + 1) * iface]
        sbuf[:, o * width : (o + 1) * width] = jnp.concatenate([piece, piece], axis=1)

    def used(g):
        return jnp.where(g < turbine_count[0], 1.0, 0.0).astype(F32)

    def inject(k, g, current, cable_half):
        strike = amp_col * (math.exp(-0.3 * k) - math.exp(-2.0 * k))
        ids = (node_row + (dev * slots + g) * nodes).astype(F32)
        struck = jnp.where(stroke_col == ids, strike, 0.0)
        value = used(g) * (current + struck + dot(cable_half, lhs[g, scens:, :]))
        lhs[g, :scens, :] = value.astype(BF16)

    def share(k, value):
        high = value.astype(BF16)
        low = (value - high.astype(F32)).astype(BF16)
        mine = gbuf.at[k - 1, :, pl.ds(pl.multiple_of(dev * width, width), width)]
        mine[...] = jnp.concatenate([high, low], axis=1)

        def one(offset, carry):
            share_copy(k, offset, dev, lax.rem(dev + offset, n_sub)).start()
            return carry

        lax.fori_loop(1, n_sub, one, 0)

    def share_copy(k, offset, owner, peer):
        ref = gbuf.at[k - 1, :, pl.ds(pl.multiple_of(owner * width, width), width)]
        return remote(ref, ref, g_send.at[k - 1, offset], g_recv.at[k - 1, offset], {"sub": peer})

    def link(k):
        def one(offset, carry):
            owner = lax.rem(dev + n_sub - offset, n_sub)
            share_copy(k, offset, owner, owner).wait_recv()
            return carry

        lax.fori_loop(1, n_sub, one, 0)
        return dot_t(gbuf[k - 1], sbuf[...]).astype(BF16)

    state_copy.wait()
    for g in range(slots):
        companion[g] = state_in[:, g, :]
    hist_send(0, left).wait_recv()
    hist_send(1, right).wait_recv()

    def past(k):
        total = jnp.zeros((scens, iface), F32)
        for back in range(depth):
            total = total + pick((hbuf[0, back], hist[back], hbuf[1, back]), k + back)
        return total

    cable_1 = -past(1)
    cable_2 = -past(2)
    cable_3 = past(3)
    cable_half = cable_1.astype(BF16)

    def start_step(g, carry):
        inject(1, g, companion[g], cable_half)
        return carry

    lax.fori_loop(0, slots, start_step, 0)
    for which, peer in enumerate((across, sib, diag)):
        pc_copy(which, peer, peer).wait_recv()
    columns = pct[...]
    for g in range(slots):
        pcb[g] = columns * (slot_col == g).astype(BF16)
    port_slot = lax.broadcasted_iota(jnp.int32, (1, iface), 1) // ports
    port_port = (dot_t(hot_all, columns) * (slot_col == port_slot).astype(F32)).astype(BF16)

    def open_ports(g, total):
        return total + dot_t(lhs[g, :scens, :], pcb[g])

    zero_ports = jnp.zeros((scens, iface), F32)
    port_1 = lax.fori_loop(0, slots, open_ports, zero_ports)
    share(1, port_1)

    def waves(k, port_open, half, cable):
        port_volt = used_row * (port_open - dot(half, port_port))
        outgoing = (used_row * (0.5 * port_volt + cable)).astype(BF16)
        wave_out[k - 1] = outgoing
        return outgoing

    half_1 = link(1)
    fbuf[2] = waves(1, port_1, half_1, cable_1)

    def fresh_send(side, peer):
        return remote(
            fbuf.at[2], fbuf.at[side], f_send.at[side], f_recv.at[side], {"sub": peer}
        )

    fresh_send(0, right).start()
    fresh_send(1, left).start()
    cable_half_2 = cable_2.astype(BF16)

    def voltage(g, value, half):
        return used(g) * (value - dot(half, prow[g]))

    def second(g, total):
        for piece in range(SPLIT):
            weight_send(0, across, g, piece).wait_recv()
            forward(g, piece).start()
        for piece in range(SPLIT):
            weight_send(1, sib, g, piece).wait_recv()
        for piece in range(SPLIT):
            forwarded(g, piece).wait_recv()
        both = dot(lhs[g], full[g])
        prow[g] = both[scens:].astype(BF16)
        volt = voltage(g, both[:scens], half_1)
        now = -companion[g] - 2.0 * gain[pl.ds(g, 1), :] * volt
        companion[g] = now
        inject(2, g, now, cable_half_2)
        return open_ports(g, total)

    port_2 = lax.fori_loop(0, slots, second, zero_ports)
    share(2, port_2)

    def multiply(g, carry):
        opened[g] = dot(lhs[g, :scens, :], full[g])
        return carry

    lax.fori_loop(0, slots, multiply, 0)
    fresh_send(0, left).wait_recv()
    fresh_send(1, right).wait_recv()
    cable_3 = -(cable_3 + pick((fbuf[0], fbuf[2], fbuf[1]), 2))
    cable_half_3 = cable_3.astype(BF16)
    half_2 = link(2)

    def third(g, total):
        volt = voltage(g, opened[g], half_2)
        now = -companion[g] - 2.0 * gain[pl.ds(g, 1), :] * volt
        inject(3, g, now, cable_half_3)
        return open_ports(g, total)

    port_3 = lax.fori_loop(0, slots, third, zero_ports)
    share(3, port_3)
    waves(2, port_2, half_2, cable_2)
    lax.fori_loop(0, slots, multiply, 0)
    half_3 = link(3)
    waves(3, port_3, half_3, cable_3)

    def finish(g, carry):
        volt_out[g] = voltage(g, opened[g], half_3).astype(BF16)
        return carry

    lax.fori_loop(0, slots, finish, 0)

    def drain_slot(g, carry):
        for piece in range(SPLIT):
            weight_send(0, across, g, piece).wait_send()
            weight_send(1, sib, g, piece).wait_send()
            forward(g, piece).wait_send()
        return carry

    lax.fori_loop(0, slots, drain_slot, 0)
    for which, peer in enumerate((across, sib, diag)):
        pc_copy(which, me, peer).wait_send()
    for side, peer in ((0, right), (1, left)):
        hist_send(side, peer).wait_send()
        fresh_send(side, peer).wait_send()

    for k in range(1, STEPS + 1):

        def drain(offset, carry, k=k):
            share_copy(k, offset, dev, lax.rem(dev + offset, n_sub)).wait_send()
            return carry

        lax.fori_loop(1, n_sub, drain, 0)


def per_device(
    n_sub,
    internal_inverse,
    schur_inverse,
    port_nodes,
    turbine_count,
    partner_port,
    cable_delay,
    history_w,
    node_state,
    node_gain,
    stroke_node,
    stroke_amp,
):
    slots, rows, nodes = internal_inverse.shape
    ports = port_nodes.shape[1]
    scens = node_state.shape[0]
    depth = history_w.shape[0]
    iface = slots * ports
    vmem = pl.BlockSpec(memory_space=pltpu.VMEM)
    smem = pl.BlockSpec(memory_space=pltpu.SMEM)
    hbm = pl.BlockSpec(memory_space=pl.ANY)
    dma = pltpu.SemaphoreType.DMA
    volt, wave = pl.pallas_call(
        functools.partial(kernel, n_sub),
        out_shape=(
            jax.ShapeDtypeStruct((slots, scens, nodes), BF16),
            jax.ShapeDtypeStruct((STEPS, scens, iface), BF16),
        ),
        in_specs=[hbm, vmem, vmem, smem, vmem, vmem, vmem, hbm, vmem, vmem, vmem],
        out_specs=(vmem, vmem),
        scratch_shapes=[
            pltpu.VMEM((slots, nodes, nodes), BF16),
            pltpu.VMEM((scens, slots, nodes), F32),
            pltpu.VMEM((slots, scens, nodes), F32),
            pltpu.VMEM((slots, scens, nodes), F32),
            pltpu.VMEM((slots, scens + iface, nodes), BF16),
            pltpu.VMEM((slots, iface, nodes), BF16),
            pltpu.VMEM((iface, nodes), BF16),
            pltpu.VMEM((slots, iface, nodes), BF16),
            pltpu.VMEM((STEPS, scens, n_sub * 2 * iface), BF16),
            pltpu.VMEM((iface, n_sub * 2 * iface), BF16),
            pltpu.VMEM((2, depth, scens, iface), BF16),
            pltpu.VMEM((3, scens, iface), BF16),
            dma(()),
            dma(()),
            dma((3, slots, SPLIT)),
            dma((3, slots, SPLIT)),
            dma((3,)),
            dma((3,)),
            dma((2,)),
            dma((2,)),
            dma((2,)),
            dma((2,)),
            dma((STEPS, n_sub)),
            dma((STEPS, n_sub)),
        ],
        compiler_params=pltpu.CompilerParams(
            collective_id=0, has_side_effects=True, vmem_limit_bytes=60 * 1024 * 1024
        ),
        name="transient",
    )(
        internal_inverse,
        schur_inverse,
        port_nodes,
        turbine_count,
        partner_port.reshape(1, iface),
        cable_delay.reshape(1, iface),
        history_w,
        node_state,
        node_gain,
        stroke_node.reshape(1, scens),
        stroke_amp.reshape(1, scens),
    )
    return jnp.swapaxes(volt, 0, 1), wave


def solution(mesh):
    return jax.shard_map(
        functools.partial(per_device, mesh.shape["sub"]),
        mesh=mesh,
        in_specs=(
            P("sub", "scen", None),
            P("sub", None),
            P("sub", None),
            P("sub"),
            P("sub"),
            P("sub"),
            P(None, "scen", "sub"),
            P("scen", "sub", None),
            P("sub", None),
            P("scen"),
            P("scen"),
        ),
        out_specs=(P("scen", "sub", None), P(None, "scen", "sub")),
        check_vma=False,
    )
```

time: 229 us -> 75.7 us (0.33)
  blocking collectives: 92.5 us -> 0 us
  Pallas kernels: 0 us -> 70.5 us
  waiting for transfers between devices: 46.5 us -> 0 us
  local copies, waits for them, and re-layouts: 30 us -> 3.66 us
  matrix products: 25.5 us -> 0 us
  between operations: 15.8 us -> 1.29 us
  starting transfers between devices: 10.9 us -> 0 us
  other arithmetic: 6.98 us -> 0 us
    all_gather x3 -> x0, blocking collectives: 92.5 us -> none  [per_device(): every_port = lax.all_gather(port_open, 'sub', axis=1, tiled=True)]
    pallas_call x0 -> x1, Pallas kernels: none -> 70.5 us  [per_device(): pl.pallas_call(functools.partial(kernel, n_sub), out_shape=(jax.ShapeDtyp...]
    all_gather x1 -> x0, waiting for transfers between devices: 43.5 us -> none  [per_device(): full_inverse = lax.all_gather(internal_inverse, 'scen', axis=1, tiled=True)]
    dot_general x12 -> x0, matrix products: 25.5 us -> none  [the longest x3 15 us: per_device(): jnp.einsum('sgm,gmn->sgn', injected, full_inverse, preferred_element_type...]
    ppermute x4 -> x0, starting transfers between devices: 10.8 us -> none  [the longest x2 8.24 us: padded(): lax.ppermute(lax.slice_in_dim(block, block.shape[dim] - width, None, axis...]
    gather x11 -> x0, local copies, waits for them, and re-layouts: 10.4 us -> none  [the longest x4 3.93 us: per_device(): jnp.take_along_axis(opened, port_nodes[None], axis=2)]
    broadcast_in_dim x16 -> x0, local copies, waits for them, and re-layouts: 7.22 us -> none  [the longest x12 5.29 us: per_device(): jnp.where((lag_time == -delay_back)[None, :], hist_cols[delay_back], 0.0)]
    mul x5 -> x0, local copies, waits for them, and re-layouts: 5.16 us -> none  [the longest x3 4.45 us: per_device(): voltage = slot_used[None, :, None] * (opened - correction)]
  transfers between devices with their start and end apart: 5 -> 0, of which waited for: 2 -> 0; matrix products, arithmetic and copies ran while one was open for 6% -> 0% of each run, Pallas kernels for 0% -> 0%
where the time goes in v1:
time: 75.7 us; the launch traced here: 75.4 us
  Pallas kernels  70.5 us (93%)
  local copies, waits for them, and re-layouts  3.66 us (5%)
  between operations  1.29 us (2%)
    pallas_call x1, Pallas kernels, per_device(): pl.pallas_call(functools.partial(kernel, n_sub), out_shape=(jax.ShapeDtyp...  70.5 us
    unnamed x2, local copies, waits for them, and re-layouts  3.66 us

profile of v1, /device:TPU:0, one launch (start us, length us, event | category | flops | bytes accessed | tf_op | source)
XLA Modules:
  0.0 75.4 jit_solution(2224642973184294938)
XLA Ops:
  1.3 70.5 %transient.1 = (bf16[4,64,1024]{2,1,0:T(8,128)(2,1)}, bf16[3,64,64]{2,1,0:T(8,128)(2,1)}) custom-call(bf16[4,256,1024]{2,1,0:T(8,128)(2,1)} %inv.1, bf16[64,512]{1,0:T(8,128)(2,1)} %schur.1, s32[4,16]{1,0:T(4,128)} %port_nodes.1, s32[1]{0:T(128)S(6)} %copy.15.turbine_count, s32[1,64]{1,0:T(1,128)} %bitcast.6, s32[1,64]{1,0:T(1,128)} %bitcast.7, ...), custom_call_target="tpu_custom_call" | custom-call | tf_op jit(solution)/shard_map/transient/pallas_call | solution.py:406
  71.8 2.2 %copy.13 = bf16[64,4,1024]{2,1,0:T(4,128)(2,1)} copy(bf16[64,4,1024]{2,0,1:T(8,128)(2,1)} %bitcast.5) | data formatting | bytes 1048576
  74.0 1.4 %copy.16 = bf16[3,64,64]{2,1,0:T(8,128)(2,1)} copy(bf16[3,64,64]{2,1,0:T(8,128)(2,1)} %get-tuple-element.11) | data formatting | bytes 49152

commit v2 on v1

--- a/solution.py
+++ b/solution.py
@@ -9,7 +9,7 @@
 from jax.sharding import PartitionSpec as P
 
 STEPS = 3
-SPLIT = 2
+SPLIT = 4
 F32 = jnp.float32
 BF16 = jnp.bfloat16
 MESH = pl.DeviceIdType.MESH
@@ -26,22 +26,32 @@
 def kernel(
     n_sub,
     inv,
+    schur_hbm,
+    port_nodes_hbm,
+    turbine_count_hbm,
+    partner_hbm,
+    delay_hbm,
+    hist_hbm,
+    node_state,
+    gain_hbm,
+    stroke_node_hbm,
+    stroke_amp_hbm,
+    volt_out,
+    wave_out,
+    full,
+    state_in,
     schur,
     port_nodes,
     turbine_count,
     partner,
     delay,
     hist,
-    node_state,
     gain,
     stroke_node,
     stroke_amp,
-    volt_out,
-    wave_out,
-    full,
-    state_in,
     companion,
     opened,
+    steady,
     lhs,
     prow,
     pct,
@@ -52,6 +62,7 @@
     fbuf,
     own_sem,
     state_sem,
+    in_sem,
     w_send,
     w_recv,
     pc_send,
@@ -78,11 +89,6 @@
     right = lax.rem(dev + 1, n_sub)
     left = lax.rem(dev + n_sub - 1, n_sub)
 
-    own_copy = pltpu.make_async_copy(inv, full.at[:, pl.ds(me * rows, rows), :], own_sem)
-    own_copy.start()
-    state_copy = pltpu.make_async_copy(node_state, state_in, state_sem)
-    state_copy.start()
-
     barrier = pltpu.get_barrier_semaphore()
     for peer in (across, sib, diag):
         pl.semaphore_signal(barrier, inc=1, device_id={"scen": peer}, device_id_type=MESH)
@@ -97,6 +103,29 @@
         return carry
 
     lax.fori_loop(1, n_sub, greet, 0)
+    own_copy = pltpu.make_async_copy(inv, full.at[:, pl.ds(me * rows, rows), :], own_sem)
+    own_copy.start()
+    state_copy = pltpu.make_async_copy(node_state, state_in, state_sem)
+    state_copy.start()
+
+    small = [
+        pltpu.make_async_copy(src, dst, in_sem.at[i])
+        for i, (src, dst) in enumerate(
+            (
+                (port_nodes_hbm, port_nodes),
+                (hist_hbm, hist),
+                (partner_hbm, partner),
+                (delay_hbm, delay),
+                (turbine_count_hbm, turbine_count),
+                (stroke_node_hbm, stroke_node),
+                (stroke_amp_hbm, stroke_amp),
+                (schur_hbm, schur),
+                (gain_hbm, gain),
+            )
+        )
+    ]
+    for copy in small:
+        copy.start()
     pl.semaphore_wait(barrier, n_sub + 2)
 
     def remote(src, dst, send, recv, peer):
@@ -146,7 +175,10 @@
             weight_send(1, sib, g, piece).start()
         return carry
 
-    weight_send(0, across, 0, 0).start()
+    for piece in range(SPLIT // 2):
+        weight_send(0, across, 0, piece).start()
+    for copy in small:
+        copy.wait()
 
     def hist_send(side, peer):
         return remote(hist, hbuf.at[side], h_send.at[side], h_recv.at[side], {"sub": peer})
@@ -186,15 +218,14 @@
 
     for which, peer in enumerate((across, sib, diag)):
         pc_copy(which, me, peer).start()
-    for piece in range(1, SPLIT):
+    for piece in range(SPLIT // 2, SPLIT):
         weight_send(0, across, 0, piece).start()
     for piece in range(SPLIT):
         weight_send(1, sib, 0, piece).start()
     lax.fori_loop(1, slots, send_slot, 0)
 
-    used_row = (
-        lax.broadcasted_iota(jnp.int32, (1, iface), 1) // ports < turbine_count[0]
-    ).astype(F32)
+    count = turbine_count[...]
+    used_row = (lax.broadcasted_iota(jnp.int32, (1, iface), 1) // ports < count).astype(F32)
     stroke_col = column(stroke_node[...].astype(F32), scens)
     amp_col = column(stroke_amp[...], scens)
     port_lane = lax.broadcasted_iota(jnp.int32, (1, iface), 1)
@@ -216,13 +247,16 @@
         sbuf[:, o * width : (o + 1) * width] = jnp.concatenate([piece, piece], axis=1)
 
     def used(g):
-        return jnp.where(g < turbine_count[0], 1.0, 0.0).astype(F32)
-
-    def inject(k, g, current, cable_half):
+        return (g < count).astype(F32)
+
+    def sources(k, g, cable_half):
         strike = amp_col * (math.exp(-0.3 * k) - math.exp(-2.0 * k))
         ids = (node_row + (dev * slots + g) * nodes).astype(F32)
         struck = jnp.where(stroke_col == ids, strike, 0.0)
-        value = used(g) * (current + struck + dot(cable_half, lhs[g, scens:, :]))
+        return struck + dot(cable_half, lhs[g, scens:, :])
+
+    def inject(k, g, current, cable_half):
+        value = used(g) * (current + sources(k, g, cable_half))
         lhs[g, :scens, :] = value.astype(BF16)
 
     def share(k, value):
@@ -308,54 +342,63 @@
     def voltage(g, value, half):
         return used(g) * (value - dot(half, prow[g]))
 
-    def second(g, total):
+    def gain_used(g):
+        return 2.0 * used(g) * gain[g : g + 1, :]
+
+    def multiply(g):
+        opened[g] = dot(lhs[g, :scens, :], full[g])
+
+    def settle(g):
+        multiply(g)
+        steady[g] = used(g) * (
+            sources(3, g, cable_half_3) - companion[g] - gain_used(g) * opened[g]
+        )
+
+    def quarter(g, owner):
+        span = pl.ds(pl.multiple_of(owner * rows, rows), rows)
+        return dot(lhs[g, :, span], full[g, span, :])
+
+    port_2 = zero_ports
+    for g in range(slots):
+        if g == 1:
+            fresh_send(0, left).wait_recv()
+            fresh_send(1, right).wait_recv()
+            cable_3 = -(cable_3 + pick((fbuf[0], fbuf[2], fbuf[1]), 2))
+            cable_half_3 = cable_3.astype(BF16)
+        if g:
+            settle(g - 1)
+        current = sources(2, g, cable_half_2) - companion[g]
+        for piece in range(SPLIT):
+            weight_send(1, sib, g, piece).wait_recv()
+        both = quarter(g, me) + quarter(g, sib)
         for piece in range(SPLIT):
             weight_send(0, across, g, piece).wait_recv()
             forward(g, piece).start()
-        for piece in range(SPLIT):
-            weight_send(1, sib, g, piece).wait_recv()
+        both = both + quarter(g, across)
         for piece in range(SPLIT):
             forwarded(g, piece).wait_recv()
-        both = dot(lhs[g], full[g])
+        both = both + quarter(g, diag)
         prow[g] = both[scens:].astype(BF16)
-        volt = voltage(g, both[:scens], half_1)
-        now = -companion[g] - 2.0 * gain[pl.ds(g, 1), :] * volt
-        companion[g] = now
-        inject(2, g, now, cable_half_2)
-        return open_ports(g, total)
-
-    port_2 = lax.fori_loop(0, slots, second, zero_ports)
+        fall = gain_used(g) * voltage(g, both[:scens], half_1)
+        lhs[g, :scens, :] = (used(g) * (current - fall)).astype(BF16)
+        companion[g] = -companion[g] - fall
+        port_2 = open_ports(g, port_2)
     share(2, port_2)
-
-    def multiply(g, carry):
-        opened[g] = dot(lhs[g, :scens, :], full[g])
-        return carry
-
-    lax.fori_loop(0, slots, multiply, 0)
-    fresh_send(0, left).wait_recv()
-    fresh_send(1, right).wait_recv()
-    cable_3 = -(cable_3 + pick((fbuf[0], fbuf[2], fbuf[1]), 2))
-    cable_half_3 = cable_3.astype(BF16)
+    settle(slots - 1)
     half_2 = link(2)
-
-    def third(g, total):
-        volt = voltage(g, opened[g], half_2)
-        now = -companion[g] - 2.0 * gain[pl.ds(g, 1), :] * volt
-        inject(3, g, now, cable_half_3)
-        return open_ports(g, total)
-
-    port_3 = lax.fori_loop(0, slots, third, zero_ports)
+    port_3 = zero_ports
+    for g in range(slots):
+        rise = used(g) * gain_used(g) * dot(half_2, prow[g])
+        lhs[g, :scens, :] = (steady[g] + rise).astype(BF16)
+        port_3 = open_ports(g, port_3)
     share(3, port_3)
     waves(2, port_2, half_2, cable_2)
-    lax.fori_loop(0, slots, multiply, 0)
+    for g in range(slots):
+        multiply(g)
     half_3 = link(3)
+    for g in range(slots):
+        volt_out[g] = voltage(g, opened[g], half_3).astype(BF16)
     waves(3, port_3, half_3, cable_3)
-
-    def finish(g, carry):
-        volt_out[g] = voltage(g, opened[g], half_3).astype(BF16)
-        return carry
-
-    lax.fori_loop(0, slots, finish, 0)
 
     def drain_slot(g, carry):
         for piece in range(SPLIT):
@@ -400,7 +443,6 @@
     depth = history_w.shape[0]
     iface = slots * ports
     vmem = pl.BlockSpec(memory_space=pltpu.VMEM)
-    smem = pl.BlockSpec(memory_space=pltpu.SMEM)
     hbm = pl.BlockSpec(memory_space=pl.ANY)
     dma = pltpu.SemaphoreType.DMA
     volt, wave = pl.pallas_call(
@@ -409,11 +451,21 @@
             jax.ShapeDtypeStruct((slots, scens, nodes), BF16),
             jax.ShapeDtypeStruct((STEPS, scens, iface), BF16),
         ),
-        in_specs=[hbm, vmem, vmem, smem, vmem, vmem, vmem, hbm, vmem, vmem, vmem],
+        in_specs=[hbm] * 11,
         out_specs=(vmem, vmem),
         scratch_shapes=[
             pltpu.VMEM((slots, nodes, nodes), BF16),
             pltpu.VMEM((scens, slots, nodes), F32),
+            pltpu.VMEM(schur_inverse.shape, BF16),
+            pltpu.VMEM((slots, ports), jnp.int32),
+            pltpu.VMEM((1, 1), jnp.int32),
+            pltpu.VMEM((1, iface), jnp.int32),
+            pltpu.VMEM((1, iface), jnp.int32),
+            pltpu.VMEM((depth, scens, iface), BF16),
+            pltpu.VMEM((slots, nodes), F32),
+            pltpu.VMEM((1, scens), jnp.int32),
+            pltpu.VMEM((1, scens), F32),
+            pltpu.VMEM((slots, scens, nodes), F32),
             pltpu.VMEM((slots, scens, nodes), F32),
             pltpu.VMEM((slots, scens, nodes), F32),
             pltpu.VMEM((slots, scens + iface, nodes), BF16),
@@ -426,6 +478,7 @@
             pltpu.VMEM((3, scens, iface), BF16),
             dma(()),
             dma(()),
+            dma((9,)),
             dma((3, slots, SPLIT)),
             dma((3, slots, SPLIT)),
             dma((3,)),
@@ -445,7 +498,7 @@
         internal_inverse,
         schur_inverse,
         port_nodes,
-        turbine_count,
+        turbine_count.reshape(1, 1),
         partner_port.reshape(1, iface),
         cable_delay.reshape(1, iface),
         history_w,

time: 75.7 us -> 74.1 us (0.979)
  Pallas kernels: 70.5 us -> 68.9 us
    pallas_call x1, Pallas kernels: 70.5 us -> 68.9 us  [per_device(): pl.pallas_call(functools.partial(kernel, n_sub), out_shape=(jax.ShapeDtyp...]
where the time goes in v2:
time: 74.1 us; the launch traced here: 73.9 us
  Pallas kernels  68.9 us (93%)
  local copies, waits for them, and re-layouts  3.66 us (5%)
  between operations  1.29 us (2%)
    pallas_call x1, Pallas kernels, per_device(): pl.pallas_call(functools.partial(kernel, n_sub), out_shape=(jax.ShapeDtyp...  68.9 us
    unnamed x2, local copies, waits for them, and re-layouts  3.66 us

profile of v2, /device:TPU:0, one launch (start us, length us, event | category | flops | bytes accessed | tf_op | source)
XLA Modules:
  0.0 73.9 jit_solution(4474094312934555570)
XLA Ops:
  1.3 68.9 %transient.1 = (bf16[4,64,1024]{2,1,0:T(8,128)(2,1)}, bf16[3,64,64]{2,1,0:T(8,128)(2,1)}) custom-call(bf16[4,256,1024]{2,1,0:T(8,128)(2,1)} %inv.1, bf16[64,512]{1,0:T(8,128)(2,1)} %schur_hbm.1, s32[4,16]{1,0:T(4,128)} %port_nodes_hbm.1, s32[1,1]{1,0:T(1,128)} %bitcast.6.turbine_count_hbm, s32[1,64]{1,0:T(1,128)} %bitcast.8, s32[1,64]{1,0:T(1,128)} %bitcast.9, ...), custom_call_target="tpu_custom_call" | custom-call | tf_op jit(solution)/shard_map/transient/pallas_call | solution.py:448
  70.2 2.2 %copy.13 = bf16[64,4,1024]{2,1,0:T(4,128)(2,1)} copy(bf16[64,4,1024]{2,0,1:T(8,128)(2,1)} %bitcast.7) | data formatting | bytes 1048576
  72.5 1.4 %copy.16 = bf16[3,64,64]{2,1,0:T(8,128)(2,1)} copy(bf16[3,64,64]{2,1,0:T(8,128)(2,1)} %get-tuple-element.11) | data formatting | bytes 49152

commit v3 on v2

--- a/solution.py
+++ b/solution.py
@@ -224,7 +224,7 @@
         weight_send(1, sib, 0, piece).start()
     lax.fori_loop(1, slots, send_slot, 0)
 
-    count = turbine_count[...]
+    count = turbine_count[0]
     used_row = (lax.broadcasted_iota(jnp.int32, (1, iface), 1) // ports < count).astype(F32)
     stroke_col = column(stroke_node[...].astype(F32), scens)
     amp_col = column(stroke_amp[...], scens)
@@ -247,7 +247,7 @@
         sbuf[:, o * width : (o + 1) * width] = jnp.concatenate([piece, piece], axis=1)
 
     def used(g):
-        return (g < count).astype(F32)
+        return jnp.where(g < count, 1.0, 0.0).astype(F32)
 
     def sources(k, g, cable_half):
         strike = amp_col * (math.exp(-0.3 * k) - math.exp(-2.0 * k))
@@ -448,8 +448,8 @@
     volt, wave = pl.pallas_call(
         functools.partial(kernel, n_sub),
         out_shape=(
-            jax.ShapeDtypeStruct((slots, scens, nodes), BF16),
-            jax.ShapeDtypeStruct((STEPS, scens, iface), BF16),
+            pltpu.VMEM((slots, scens, nodes), BF16),
+            pltpu.VMEM((STEPS, scens, iface), BF16),
         ),
         in_specs=[hbm] * 11,
         out_specs=(vmem, vmem),
@@ -458,7 +458,7 @@
             pltpu.VMEM((scens, slots, nodes), F32),
             pltpu.VMEM(schur_inverse.shape, BF16),
             pltpu.VMEM((slots, ports), jnp.int32),
-            pltpu.VMEM((1, 1), jnp.int32),
+            pltpu.SMEM((1,), jnp.int32),
             pltpu.VMEM((1, iface), jnp.int32),
             pltpu.VMEM((1, iface), jnp.int32),
             pltpu.VMEM((depth, scens, iface), BF16),
@@ -498,7 +498,7 @@
         internal_inverse,
         schur_inverse,
         port_nodes,
-        turbine_count.reshape(1, 1),
+        turbine_count,
         partner_port.reshape(1, iface),
         cable_delay.reshape(1, iface),
         history_w,

time: 74.1 us -> 71.4 us (0.964)
  local copies, waits for them, and re-layouts: 3.66 us -> 1.82 us
  Pallas kernels: 68.9 us -> 68.1 us
    unnamed x2, local copies, waits for them, and re-layouts: 3.66 us -> 1.82 us
    pallas_call x1, Pallas kernels: 68.9 us -> 68.1 us  [per_device(): pl.pallas_call(functools.partial(kernel, n_sub), out_shape=(pltpu.VMEM((s...]
where the time goes in v3:
time: 71.4 us; the launch traced here: 71.2 us
  Pallas kernels  68.1 us (95%)
  local copies, waits for them, and re-layouts  1.82 us (3%)
  between operations  1.29 us (2%)
    pallas_call x1, Pallas kernels, per_device(): pl.pallas_call(functools.partial(kernel, n_sub), out_shape=(pltpu.VMEM((s...  68.1 us
    unnamed x2, local copies, waits for them, and re-layouts  1.82 us

profile of v3, /device:TPU:0, one launch (start us, length us, event | category | flops | bytes accessed | tf_op | source)
XLA Modules:
  0.0 71.2 jit_solution(18007251766445301632)
XLA Ops:
  1.3 68.1 %transient.1 = (bf16[4,64,1024]{2,1,0:T(8,128)(2,1)S(1)}, bf16[3,64,64]{2,1,0:T(8,128)(2,1)S(1)}) custom-call(bf16[4,256,1024]{2,1,0:T(8,128)(2,1)} %inv.1, bf16[64,512]{1,0:T(8,128)(2,1)} %schur_hbm.1, s32[4,16]{1,0:T(4,128)} %port_nodes_hbm.1, s32[1]{0:T(128)S(6)} %copy.16.turbine_count_hbm, s32[1,64]{1,0:T(1,128)} %bitcast.6, s32[1,64]{1,0:T(1,128)} %bitcast.7, ...), custom_call_target="tpu_custom_call" | custom-call | tf_op jit(solution)/shard_map/transient/pallas_call | solution.py:448
  69.4 1.2 %copy.13 = bf16[64,4,1024]{2,1,0:T(4,128)(2,1)} copy(bf16[64,4,1024]{2,0,1:T(8,128)(2,1)S(1)} %bitcast.5) | data formatting | bytes 1048576
  70.6 0.6 copy.15

commit v4 on v3

--- a/solution.py
+++ b/solution.py
@@ -9,7 +9,7 @@
 from jax.sharding import PartitionSpec as P
 
 STEPS = 3
-SPLIT = 4
+SPLIT = 2
 F32 = jnp.float32
 BF16 = jnp.bfloat16
 MESH = pl.DeviceIdType.MESH

time: 71.4 us -> 70.8 us (level)
  no operation moved by 1% of the time
where the time goes in v4:
time: 70.8 us; the launch traced here: 70.6 us
  Pallas kernels  67.5 us (95%)
  local copies, waits for them, and re-layouts  1.82 us (3%)
  between operations  1.29 us (2%)
    pallas_call x1, Pallas kernels, per_device(): pl.pallas_call(functools.partial(kernel, n_sub), out_shape=(pltpu.VMEM((s...  67.5 us
    unnamed x2, local copies, waits for them, and re-layouts  1.82 us

profile of v4, /device:TPU:0, one launch (start us, length us, event | category | flops | bytes accessed | tf_op | source)
XLA Modules:
  0.0 70.6 jit_solution(18291980713680671581)
XLA Ops:
  1.3 67.5 %transient.1 = (bf16[4,64,1024]{2,1,0:T(8,128)(2,1)S(1)}, bf16[3,64,64]{2,1,0:T(8,128)(2,1)S(1)}) custom-call(bf16[4,256,1024]{2,1,0:T(8,128)(2,1)} %inv.1, bf16[64,512]{1,0:T(8,128)(2,1)} %schur_hbm.1, s32[4,16]{1,0:T(4,128)} %port_nodes_hbm.1, s32[1]{0:T(128)S(6)} %copy.16.turbine_count_hbm, s32[1,64]{1,0:T(1,128)} %bitcast.6, s32[1,64]{1,0:T(1,128)} %bitcast.7, ...), custom_call_target="tpu_custom_call" | custom-call | tf_op jit(solution)/shard_map/transient/pallas_call | solution.py:448
  68.8 1.2 %copy.13 = bf16[64,4,1024]{2,1,0:T(4,128)(2,1)} copy(bf16[64,4,1024]{2,0,1:T(8,128)(2,1)S(1)} %bitcast.5) | data formatting | bytes 1048576
  70.0 0.6 copy.15
